TPU v7x, 128 devices: a whole 4x4x4 slice. The times are simulated.
128 devices in a mesh: dp: 8 (over x, core), space: 16 (over z, y).
Axes of the slice: x: 4, y: 4, z: 4, core: 2. Of those that a mesh axis runs over, the one named last changes fastest.
Arguments:
- features: bfloat16 [8, 192, 72, 2048], P('dp', 'space'), may hold values from -0.10205078 to 0.10205078
- grad_out: bfloat16 [8, 192, 72, 256], P('dp', 'space'), may hold values from -6 to 6
- weight: bfloat16 [18432, 256], replicated, may hold values from -0.125 to 0.125
- alive: int32 [8], P('dp'), may hold values from 0 to 1, as said below
Outputs:
- weight_grad: float32 [18432, 256], P(('dp', 'space'))
- grad_features: bfloat16 [8, 192, 72, 2048], P('dp', 'space')
Inputs may be any that keep to these rules, and one draw needn't show every extreme that they name: `alive`: at least one member survives and at least one does not.
All inputs are finite; a program needn't handle non-finite values.
Results may differ from a plain program's by a relative error of at most 0.001.
Values may be sent and summed in bfloat16 or wider, within the bound.
A program may use at most 320 MiB of HBM per device.

v0:
```python
import jax
import jax.numpy as jnp
from jax import lax
from jax.sharding import PartitionSpec as P

KERNEL_DILATION = 18


def from_behind(value, axis, steps):
    count = lax.axis_size(axis)
    leading, last = (max(0, -steps), min(count, count - steps))
    return lax.ppermute(value, axis, [(source, source + steps) for source in range(leading, last)])


def widen_cols(climate_field):
    return jnp.pad(climate_field, ((0, 0), (0, 0), (KERNEL_DILATION, KERNEL_DILATION), (0, 0)))


def grad_rows(tile):
    rows_per_tile = tile.shape[1]
    halo_tile_count = -(-KERNEL_DILATION // rows_per_tile)
    above_rows = []
    below_rows = []
    for tap_displacement in range(1, halo_tile_count + 1):
        required_rows = min(rows_per_tile, KERNEL_DILATION - (tap_displacement - 1) * rows_per_tile)
        above_rows.insert(
            0, from_behind(tile[:, rows_per_tile - required_rows :], "space", tap_displacement)
        )
        below_rows.append(from_behind(tile[:, :required_rows], "space", -tap_displacement))
    return jnp.concatenate(above_rows + [tile] + below_rows, axis=1)


def feature_rows(tile):
    rows_per_tile = tile.shape[1]
    halo_tile_count = -(-KERNEL_DILATION // rows_per_tile)
    above_rows = []
    below_rows = []
    for tap_displacement in range(1, halo_tile_count + 1):
        required_rows = min(rows_per_tile, KERNEL_DILATION - (tap_displacement - 1) * rows_per_tile)
        above_rows.insert(
            0, from_behind(tile[:, rows_per_tile - required_rows :], "space", tap_displacement)
        )
        below_rows.append(from_behind(tile[:, :required_rows], "space", -tap_displacement))
    return jnp.concatenate(above_rows + [tile] + below_rows, axis=1)


def tap_stack(padded, row_count, col_count, forward):
    views = []
    for tap_index in range(9):
        kernel_tap_row = tap_index // 3
        kernel_tap_column = tap_index % 3
        if forward:
            row_position = kernel_tap_row * KERNEL_DILATION
            column_position = kernel_tap_column * KERNEL_DILATION
        else:
            row_position = (2 - kernel_tap_row) * KERNEL_DILATION
            column_position = (2 - kernel_tap_column) * KERNEL_DILATION
        views.append(
            padded[
                :,
                row_position : row_position + row_count,
                column_position : column_position + col_count,
            ]
        )
    return jnp.stack(views, axis=3)


def shards(features, grad_out, weight, alive):
    members, rows_per_tile, map_width, in_channels = features.shape
    out_channels = grad_out.shape[-1]
    surviving_count = lax.psum(jnp.sum(alive).astype(jnp.float32), "dp")
    member_weighting = alive.astype(jnp.float32) / surviving_count
    pixels = rows_per_tile * map_width
    tap_weights = weight.reshape(in_channels, 9, out_channels)
    gradient_padded = widen_cols(grad_rows(grad_out))
    shifted = tap_stack(gradient_padded, rows_per_tile, map_width, False).reshape(
        members, pixels, 9, out_channels
    )
    input_grad = jnp.einsum(
        "mpto,cto->mpc", shifted, tap_weights, preferred_element_type=jnp.float32
    )
    grad_features = (
        (input_grad * member_weighting[:, None, None]).astype(jnp.bfloat16).reshape(features.shape)
    )
    image_padded = widen_cols(feature_rows(features))
    flat_grad = grad_out.reshape(members, pixels, out_channels)
    rows_total = 9 * in_channels
    chan_count = rows_total // lax.axis_size(("dp", "space")) * lax.axis_size(("dp", "space")) // 9
    stacked = tap_stack(image_padded, rows_per_tile, map_width, True).reshape(
        members, pixels, 9, chan_count
    )
    term = jnp.einsum("mptc,mpo->mcto", stacked, flat_grad, preferred_element_type=jnp.float32)
    weighted = jnp.einsum("mcto,m->cto", term, member_weighting)
    weight_grad = lax.psum_scatter(
        weighted.reshape(chan_count * 9, out_channels),
        ("dp", "space"),
        scatter_dimension=0,
        tiled=True,
    )
    return (weight_grad, grad_features)


def solution(mesh):
    in_specs = (P("dp", "space", None, None), P("dp", "space", None, None), P(), P("dp"))
    out_specs = (P(("dp", "space"), None), P("dp", "space", None, None))
    return jax.shard_map(shards, mesh=mesh, in_specs=in_specs, out_specs=out_specs, check_vma=False)
```

profile of v0, /device:TPU:0, one launch (start us, length us, event | category | flops | bytes accessed | tf_op | source)
XLA Modules:
  0.0 524.6 jit_solution(12726439417157724754)
XLA Ops:
  7.2 5.4 %collective-permute-start.1 = (bf16[1,12,72,2048]{3,2,1,0:T(8,128)(2,1)}, bf16[1,12,72,2048]{3,2,1,0:T(8,128)(2,1)}, u32[]{:S(2)}, u32[]{:S(2)}) collective-permute-start(bf16[1,12,72,2048]{3,2,1,0:T(8,128)(2,1)} %param.4), channel_id=1, source_target_pairs={{0,1},{1,2},{2,3},{3,4},{4,5},{5,6},{6,7},{7,8},{8,9},{9,10},{10,1... | collective-permute-start | bytes 10616840 | tf_op jit(solution)/shard_map/ppermute | solution.py:12
  13.9 3.6 fusion.12
  17.5 5.6 %collective-permute-start = (bf16[1,6,72,2048]{3,2,1,0:T(8,128)(2,1)S(1)}, bf16[1,6,72,2048]{3,2,1,0:T(8,128)(2,1)}, u32[]{:S(2)}, u32[]{:S(2)}) collective-permute-start(bf16[1,6,72,2048]{3,2,1,0:T(8,128)(2,1)S(1)} %get-tuple-element.13), channel_id=1, source_target_pairs={{0,2},{1,3},{2,4},{3,5},{4,6},{5,7},{6,8},{7,9},{8,10},{9,11},{10,... | collective-permute-start | bytes 5308424 | tf_op jit(solution)/shard_map/ppermute | solution.py:12
  25.0 14.3 %psum.7 = f32[1]{0:T(128)} all-reduce(f32[1]{0:T(128)S(6)} %convert_element_type.15), channel_id=1, replica_groups=mesh['dp'=8,'space'=16] {'dp'}, use_global_device_ids=true, to_apply=%region_0.0 | all-reduce | flops 1 | bytes 8 | tf_op jit(solution)/shard_map/psum | solution.py:71
  40.0 84.7 %collective-permute-done = bf16[1,6,72,2048]{3,2,1,0:T(8,128)(2,1)} collective-permute-done((bf16[1,6,72,2048]{3,2,1,0:T(8,128)(2,1)S(1)}, bf16[1,6,72,2048]{3,2,1,0:T(8,128)(2,1)}, u32[]{:S(2)}, u32[]{:S(2)}) %collective-permute-start) | collective-permute-done | bytes 1769504 | tf_op jit(solution)/shard_map/ppermute | solution.py:12
  124.7 1.6 constant_dynamic-update-slice_fusion.4
  126.3 4.8 pad_maximum_fusion.1
  132.0 34.2 %collective-permute-done.3 = bf16[1,6,72,2048]{3,2,1,0:T(8,128)(2,1)} collective-permute-done((bf16[1,6,72,2048]{3,2,1,0:T(8,128)(2,1)}, bf16[1,6,72,2048]{3,2,1,0:T(8,128)(2,1)}, u32[]{:S(2)}, u32[]{:S(2)}) %collective-permute-start.3) | collective-permute-done | bytes 1769504 | tf_op jit(solution)/shard_map/ppermute | solution.py:12
  166.2 4.8 pad_maximum_fusion
  170.9 1.6 constant_dynamic-update-slice_fusion
  172.5 8.5 %pad_slice_fusion = (bf16[1,12,72,2048]{3,2,1,0:T(8,128)(2,1)S(1)}, bf16[1,12,72,2048]{3,2,1,0:T(8,128)(2,1)}, bf16[1,12,72,2048]{3,2,1,0:T(8,128)(2,1)}, bf16[1...) fusion(bf16[1,48,72,2048]{3,2,1,0:T(8,128)(2,1)S(1)} %constant_dynamic-update, ...), kind=kLoop, calls=%fused_computation.2 | loop fusion | bytes 35389440 | tf_op jit(solution)/shard_map/slice | solution.py:59
  181.1 4.4 constant_dynamic-update-slice_fusion.13
  185.5 2.2 constant_dynamic-update-slice_fusion.12
  188.7 2.3 constant_dynamic-update-slice_fusion.11
  191.0 2.3 constant_dynamic-update-slice_fusion.10
  193.3 2.1 constant_dynamic-update-slice_fusion.9
  196.6 2.2 constant_dynamic-update-slice_fusion.8
  198.8 2.1 constant_dynamic-update-slice_fusion.7
  202.1 2.1 constant_dynamic-update-slice_fusion.6
  204.2 2.1 constant_dynamic-update-slice_fusion.5
  206.3 19.6 %multiply_bitcast_fusion = f32[1,2048,9,256]{3,1,2,0:T(8,128)} fusion(f32[]{:T(128)} %bitcast.12, bf16[864,256,1]{1,0,2:T(8,128)(2,1)S(1)} %bitcast.53, bf16[1,864,9,2048]{3,1,2,0:T(8,128)(2,1)} %constant_dynamic-update-slice_fusion.5), kind=kOutput, calls=%fused_computation.8 | convolution fusion | flops 8158445568 | bytes 51167236 | tf_op jit(solution)/shard_map/mptc,mpo->mcto/dot_general | solution.py:92
  225.9 23.3 %copy.7 = f32[1,2048,9,256]{3,2,1,0:T(8,128)} copy(f32[1,2048,9,256]{3,1,2,0:T(8,128)} %multiply_bitcast_fusion) | data formatting | bytes 37748736 | tf_op jit(solution)/shard_map/mcto,m->cto/dot_general | solution.py:93
  249.2 26.4 %dot_general.25 = f32[18432,256]{1,0:T(8,128)} reshape(f32[1,2048,9,256]{3,2,1,0:T(8,128)} %copy.7) | data formatting | bytes 37748736 | tf_op jit(solution)/shard_map/mcto,m->cto/dot_general | solution.py:93
  275.7 5.6 %collective-permute-start.5 = (bf16[1,12,72,256]{3,2,1,0:T(8,128)(2,1)S(1)}, bf16[1,12,72,256]{3,2,1,0:T(8,128)(2,1)}, u32[]{:S(2)}, u32[]{:S(2)}) collective-permute-start(bf16[1,12,72,256]{3,2,1,0:T(8,128)(2,1)S(1)} %copy-done.7), channel_id=1, source_target_pairs={{0,1},{1,2},{2,3},{3,4},{4,5},{5,6},{6,7},{7,8},{8,9},{9,10},{10,1... | collective-permute-start | bytes 1327112 | tf_op jit(solution)/shard_map/ppermute | solution.py:12
  282.0 5.4 %collective-permute-start.4 = (bf16[1,6,72,256]{3,2,1,0:T(8,128)(2,1)S(1)}, bf16[1,6,72,256]{3,2,1,0:T(8,128)(2,1)S(1)}, u32[]{:S(2)}, u32[]{:S(2)}) collective-permute-start(bf16[1,6,72,256]{3,2,1,0:T(8,128)(2,1)S(1)} %get-tuple-element.25), channel_id=1, source_target_pairs={{0,2},{1,3},{2,4},{3,5},{4,6},{5,7},{6,8},{7,9},{8,10},{9,11},{10,... | collective-permute-start | bytes 663560 | tf_op jit(solution)/shard_map/ppermute | solution.py:12
  287.5 1.3 collective-permute-start.6
  288.8 1.3 collective-permute-start.7
  290.1 18.6 %reshape.84 = bf16[2048,9,256]{2,1,0:T(8,128)(2,1)} reshape(bf16[18432,256]{1,0:T(8,128)(2,1)} %param.6) | data formatting | bytes 18874368 | tf_op jit(solution)/shard_map/reshape | solution.py:74
  308.7 1.4 pad_maximum_fusion.2
  310.2 1.6 pad_maximum_fusion.3
  320.2 16.2 %fusion.4 = bf16[864,2048]{1,0:T(8,128)(2,1)} fusion(bf16[2048,9,256]{2,1,0:T(8,128)(2,1)S(1)} %copy-done.1, bf16[1,864,9,256]{3,1,2,0:T(8,128)(2,1)} %constant_dynamic-update-slice_fusion.19, f32[]{:T(128)} %bitcast.12), kind=kOutput, calls=%fused_computation.12 | convolution fusion | flops 8157265920 | bytes 16957444 | tf_op jit(solution)/shard_map/mpto,cto->mpc/dot_general | solution.py:79
  336.4 181.4 %reduce-scatter.2.cloned.1.call-done = f32[144,256]{1,0:T(8,128)} async-done(((f32[18432,256]{1,0:T(8,128)}), f32[144,256]{1,0:T(8,128)}) %reduce-scatter.2.cloned.1.call-update) | async-done | bytes 147472 | tf_op jit(solution)/shard_map/reduce_scatter | solution.py:94
  (41 shorter events, 16.2 us)
Async XLA Ops:
  7.2 510.6 %reduce-scatter.2.cloned.1.call-start = ((), (), s32[]{:S(2)}) async-start(), calls=%async_computation.1 | async-start | bytes 19021824 | tf_op jit(solution)/shard_map/reduce_scatter | solution.py:94
  7.2 119.1 %collective-permute-start.1 = (bf16[1,12,72,2048]{3,2,1,0:T(8,128)(2,1)}, bf16[1,12,72,2048]{3,2,1,0:T(8,128)(2,1)}, u32[]{:S(2)}, u32[]{:S(2)}) collective-permute-start(bf16[1,12,72,2048]{3,2,1,0:T(8,128)(2,1)} %param.4), channel_id=1, source_target_pairs={{0,1},{1,2},{2,3},{3,4},{4,5},{5,6},{6,7},{7,8},{8,9},{9,10},{10,1... | collective-permute-start | bytes 10616840 | tf_op jit(solution)/shard_map/ppermute | solution.py:12
  12.6 153.6 %collective-permute-start.2 = (bf16[1,12,72,2048]{3,2,1,0:T(8,128)(2,1)}, bf16[1,12,72,2048]{3,2,1,0:T(8,128)(2,1)}, u32[]{:S(2)}, u32[]{:S(2)}) collective-permute-start(bf16[1,12,72,2048]{3,2,1,0:T(8,128)(2,1)} %param.4), channel_id=1, source_target_pairs={{1,0},{2,1},{3,2},{4,3},{5,4},{6,5},{7,6},{8,7},{9,8},{10,9},{11,1... | collective-permute-start | bytes 10616840 | tf_op jit(solution)/shard_map/ppermute | solution.py:12
  17.5 107.3 %collective-permute-start = (bf16[1,6,72,2048]{3,2,1,0:T(8,128)(2,1)S(1)}, bf16[1,6,72,2048]{3,2,1,0:T(8,128)(2,1)}, u32[]{:S(2)}, u32[]{:S(2)}) collective-permute-start(bf16[1,6,72,2048]{3,2,1,0:T(8,128)(2,1)S(1)} %get-tuple-element.13), channel_id=1, source_target_pairs={{0,2},{1,3},{2,4},{3,5},{4,6},{5,7},{6,8},{7,9},{8,10},{9,11},{10,... | collective-permute-start | bytes 5308424 | tf_op jit(solution)/shard_map/ppermute | solution.py:12
  23.1 143.1 %collective-permute-start.3 = (bf16[1,6,72,2048]{3,2,1,0:T(8,128)(2,1)}, bf16[1,6,72,2048]{3,2,1,0:T(8,128)(2,1)}, u32[]{:S(2)}, u32[]{:S(2)}) collective-permute-start(bf16[1,6,72,2048]{3,2,1,0:T(8,128)(2,1)} %get-tuple-element.12), channel_id=1, source_target_pairs={{2,0},{3,1},{4,2},{5,3},{6,4},{7,5},{8,6},{9,7},{10,8},{11,9},{12,... | collective-permute-start | bytes 5308424 | tf_op jit(solution)/shard_map/ppermute | solution.py:12
  126.3 5.2 copy-start
  181.1 4.4 copy-start.6
  185.5 3.3 copy-start.4
  187.7 3.3 copy-start.3
  193.3 3.3 copy-start.2
  198.8 3.3 copy-start.5
  204.2 2.1 copy-start.7
  275.7 33.1 %collective-permute-start.5 = (bf16[1,12,72,256]{3,2,1,0:T(8,128)(2,1)S(1)}, bf16[1,12,72,256]{3,2,1,0:T(8,128)(2,1)}, u32[]{:S(2)}, u32[]{:S(2)}) collective-permute-start(bf16[1,12,72,256]{3,2,1,0:T(8,128)(2,1)S(1)} %copy-done.7), channel_id=1, source_target_pairs={{0,1},{1,2},{2,3},{3,4},{4,5},{5,6},{6,7},{7,8},{8,9},{9,10},{10,1... | collective-permute-start | bytes 1327112 | tf_op jit(solution)/shard_map/ppermute | solution.py:12
  282.0 26.7 %collective-permute-start.4 = (bf16[1,6,72,256]{3,2,1,0:T(8,128)(2,1)S(1)}, bf16[1,6,72,256]{3,2,1,0:T(8,128)(2,1)S(1)}, u32[]{:S(2)}, u32[]{:S(2)}) collective-permute-start(bf16[1,6,72,256]{3,2,1,0:T(8,128)(2,1)S(1)} %get-tuple-element.25), channel_id=1, source_target_pairs={{0,2},{1,3},{2,4},{3,5},{4,6},{5,7},{6,8},{7,9},{8,10},{9,11},{10,... | collective-permute-start | bytes 663560 | tf_op jit(solution)/shard_map/ppermute | solution.py:12
  287.5 22.7 %collective-permute-start.6 = (bf16[1,12,72,256]{3,2,1,0:T(8,128)(2,1)S(1)}, bf16[1,12,72,256]{3,2,1,0:T(8,128)(2,1)}, u32[]{:S(2)}, u32[]{:S(2)}) collective-permute-start(bf16[1,12,72,256]{3,2,1,0:T(8,128)(2,1)S(1)} %copy-done.7), channel_id=1, source_target_pairs={{1,0},{2,1},{3,2},{4,3},{5,4},{6,5},{7,6},{8,7},{9,8},{10,9},{11,1... | collective-permute-start | bytes 1327112 | tf_op jit(solution)/shard_map/ppermute | solution.py:12
  288.8 21.4 %collective-permute-start.7 = (bf16[1,6,72,256]{3,2,1,0:T(8,128)(2,1)}, bf16[1,6,72,256]{3,2,1,0:T(8,128)(2,1)S(1)}, u32[]{:S(2)}, u32[]{:S(2)}) collective-permute-start(bf16[1,6,72,256]{3,2,1,0:T(8,128)(2,1)} %get-tuple-element.24), channel_id=1, source_target_pairs={{2,0},{3,1},{4,2},{5,3},{6,4},{7,5},{8,6},{9,7},{10,8},{11,9},{12,... | collective-permute-start | bytes 663560 | tf_op jit(solution)/shard_map/ppermute | solution.py:12
  308.7 11.5 %copy-start.1 = (bf16[2048,9,256]{2,1,0:T(8,128)(2,1)S(1)}, bf16[2048,9,256]{2,1,0:T(8,128)(2,1)}, u32[]{:S(2)}) copy-start(bf16[2048,9,256]{2,1,0:T(8,128)(2,1)} %reshape.84) | copy-start | bytes 28311556
Sparse Core Ops, SparseCore 0:
  275.8 241.9 reduce-scatter.1
where the time goes:
time: 526 us; the launch traced here: 525 us
  waiting for transfers between devices  300 us (57%)
  local copies, waits for them, and re-layouts  119 us (23%)
  matrix products  35.8 us (7%)
  starting transfers between devices  27.2 us (5%)
  between operations  15.5 us (3%)
  blocking collectives  14.3 us (3%)
  other arithmetic  12.5 us (2%)
    reduce_scatter x1, waiting for transfers between devices, shards(): lax.psum_scatter(weighted.reshape(chan_count * 9, out_channels), ('dp', '...  181 us
    ppermute x8, waiting for transfers between devices, from_behind(): lax.ppermute(value, axis, [(source, source + steps) for source in range(l...  119 us
    dot_general x2, local copies, waits for them, and re-layouts, shards(): weighted = jnp.einsum('mcto,m->cto', term, member_weighting)  49.7 us
    unnamed x36, local copies, waits for them, and re-layouts  32 us
    ppermute x8, starting transfers between devices, from_behind(): lax.ppermute(value, axis, [(source, source + steps) for source in range(l...  27.2 us
    dot_general x1, matrix products, shards(): jnp.einsum('mptc,mpo->mcto', stacked, flat_grad, preferred_element_type=j...  19.6 us
    reshape x1, local copies, waits for them, and re-layouts, shards(): tap_weights = weight.reshape(in_channels, 9, out_channels)  18.6 us
    dot_general x1, matrix products, shards(): jnp.einsum('mpto,cto->mpc', shifted, tap_weights, preferred_element_type=...  16.2 us
  transfers between devices with their start and end apart: 9, of which 3 were waited for; matrix products, arithmetic and copies ran while one was open for 11% of the time, Pallas kernels for 0%

commit v1 on v0

v1 whole, which is shorter than its diff:
```python
import jax
import jax.numpy as jnp
from jax import lax
from jax.sharding import PartitionSpec as P

KERNEL_DILATION = 18


def from_behind(value, axis, steps):
    count = lax.axis_size(axis)
    leading, last = (max(0, -steps), min(count, count - steps))
    return lax.ppermute(value, axis, [(source, source + steps) for source in range(leading, last)])


def shifted_rows(tile):
    rows = tile.shape[1]
    lag, extra = divmod(KERNEL_DILATION, rows)
    keep = rows - extra
    above, below = [], []
    if extra:
        above.append(from_behind(tile[:, keep:], "space", lag + 1))
    above.append(from_behind(tile[:, :keep], "space", lag))
    below.append(from_behind(tile[:, extra:], "space", -lag))
    if extra:
        below.append(from_behind(tile[:, :extra], "space", -(lag + 1)))
    return jnp.concatenate(above, axis=1), jnp.concatenate(below, axis=1)


def tap_matrix(grad):
    members, rows, cols, out_channels = grad.shape
    above, below = shifted_rows(grad)
    blocks = []
    for source in (below, grad, above):
        wide = jnp.pad(source, ((0, 0), (0, 0), (KERNEL_DILATION, KERNEL_DILATION), (0, 0)))
        for kx in range(3):
            start = (2 - kx) * KERNEL_DILATION
            blocks.append(wide[:, :, start : start + cols])
    return jnp.concatenate(blocks, axis=-1).reshape(members * rows * cols, 9 * out_channels)


def shards(features, grad_out, weight, alive):
    members, rows, cols, in_channels = features.shape
    out_channels = grad_out.shape[-1]
    survivors = lax.psum(jnp.sum(alive).astype(jnp.float32), "dp")
    scale = (alive.astype(jnp.float32) / survivors)[0]
    taps = tap_matrix(grad_out)
    flat = features.reshape(rows * cols, in_channels)
    term = lax.dot_general(flat, taps, (((0,), (0,)), ((), ())), preferred_element_type=jnp.float32)
    mine = lax.psum_scatter(term * scale, ("dp", "space"), scatter_dimension=0, tiled=True)
    weight_grad = mine.reshape(-1, out_channels)
    kernel = weight.reshape(in_channels, 9 * out_channels)
    back = lax.dot_general(taps, kernel, (((1,), (1,)), ((), ())), preferred_element_type=jnp.float32)
    grad_features = (back * scale).astype(jnp.bfloat16).reshape(features.shape)
    return weight_grad, grad_features


def solution(mesh):
    in_specs = (P("dp", "space", None, None), P("dp", "space", None, None), P(), P("dp"))
    out_specs = (P(("dp", "space"), None), P("dp", "space", None, None))
    return jax.shard_map(shards, mesh=mesh, in_specs=in_specs, out_specs=out_specs, check_vma=False)
```

time: 526 us -> 328 us (0.62)
  waiting for transfers between devices: 300 us -> 207 us
  local copies, waits for them, and re-layouts: 119 us -> 46 us
  starting transfers between devices: 27.2 us -> 14.6 us
  other arithmetic: 12.5 us -> 2.35 us
  matrix products: 35.8 us -> 26.9 us
    ppermute x8 -> x4, waiting for transfers between devices: 119 us -> 0.01 us  [from_behind(): lax.ppermute(value, axis, [(source, source + steps) for source in range(l...]
    dot_general x2 -> x0, local copies, waits for them, and re-layouts: 49.7 us -> none  [shards(): weighted = jnp.einsum('mcto,m->cto', term, member_weighting)]
    reduce_scatter x1, waiting for transfers between devices: 181 us -> 207 us  [shards(): lax.psum_scatter(term * scale, ('dp', 'space'), scatter_dimension=0, tile...]
    ppermute x8 -> x4, starting transfers between devices: 27.2 us -> 14.6 us  [from_behind(): lax.ppermute(value, axis, [(source, source + steps) for source in range(l...]
    slice x4 -> x1, local copies, waits for them, and re-layouts: 14.1 us -> 1.97 us  [shifted_rows(): below.append(from_behind(tile[:, extra:], 'space', -lag))]
    concatenate x4 -> x2, other arithmetic: 12.5 us -> 2.35 us  [shifted_rows(): return (jnp.concatenate(above, axis=1), jnp.concatenate(below, axis=1))]
    dot_general x2, matrix products: 35.8 us -> 26.9 us  [the longest x1 13.7 us: shards(): lax.dot_general(taps, kernel, (((1,), (1,)), ((), ())), preferred_element...]
    unnamed x36 -> x19, local copies, waits for them, and re-layouts: 32 us -> 24.8 us
  transfers between devices with their start and end apart: 9 -> 5, of which waited for: 3 -> 1; matrix products, arithmetic and copies ran while one was open for 11% -> 11% of each run, Pallas kernels for 0% -> 0%
where the time goes in v1:
time: 328 us; the launch traced here: 327 us
  waiting for transfers between devices  207 us (63%)
  local copies, waits for them, and re-layouts  46 us (14%)
  matrix products  26.9 us (8%)
  between operations  15.6 us (5%)
  starting transfers between devices  14.6 us (4%)
  blocking collectives  14.1 us (4%)
    reduce_scatter x1, waiting for transfers between devices, shards(): lax.psum_scatter(term * scale, ('dp', 'space'), scatter_dimension=0, tile...  207 us
    unnamed x19, local copies, waits for them, and re-layouts  24.8 us
    reshape x1, local copies, waits for them, and re-layouts, shards(): kernel = weight.reshape(in_channels, 9 * out_channels)  17.5 us
    ppermute x4, starting transfers between devices, from_behind(): lax.ppermute(value, axis, [(source, source + steps) for source in range(l...  14.6 us
    psum x1, blocking collectives, shards(): survivors = lax.psum(jnp.sum(alive).astype(jnp.float32), 'dp')  14.1 us
    dot_general x1, matrix products, shards(): lax.dot_general(taps, kernel, (((1,), (1,)), ((), ())), preferred_element...  13.7 us
    dot_general x1, matrix products, shards(): lax.dot_general(flat, taps, (((0,), (0,)), ((), ())), preferred_element_t...  13.2 us
  transfers between devices with their start and end apart: 5, of which 1 were waited for; matrix products, arithmetic and copies ran while one was open for 11% of the time, Pallas kernels for 0%

profile of v1, /device:TPU:0, one launch (start us, length us, event | category | flops | bytes accessed | tf_op | source)
XLA Modules:
  0.0 326.7 jit_solution(7894516058408091715)
XLA Ops:
  7.2 0.0 copy-start
  7.2 0.0 reduce-scatter.4.cloned.1.call-start
  7.2 2.0 fusion.9
  9.2 1.3 collective-permute-start
  10.5 1.3 collective-permute-start.1
  11.8 7.6 %collective-permute-start.2 = (bf16[1,6,72,256]{3,2,1,0:T(8,128)(2,1)}, bf16[1,6,72,256]{3,2,1,0:T(8,128)(2,1)}, u32[]{:S(2)}, u32[]{:S(2)}) collective-permute-start(bf16[1,6,72,256]{3,2,1,0:T(8,128)(2,1)} %get-tuple-element.2), channel_id=1, source_target_pairs={{0,2},{1,3},{2,4},{3,5},{4,6},{5,7},{6,8},{7,9},{8,10},{9,11},{10,... | collective-permute-start | bytes 663560 | tf_op jit(solution)/shard_map/ppermute | solution.py:12
  20.0 4.4 %collective-permute-start.3 = (bf16[1,6,72,256]{3,2,1,0:T(8,128)(2,1)}, bf16[1,6,72,256]{3,2,1,0:T(8,128)(2,1)}, u32[]{:S(2)}, u32[]{:S(2)}) collective-permute-start(bf16[1,6,72,256]{3,2,1,0:T(8,128)(2,1)} %get-tuple-element.3), channel_id=1, source_target_pairs={{0,1},{1,2},{2,3},{3,4},{4,5},{5,6},{6,7},{7,8},{8,9},{9,10},{10,1... | collective-permute-start | bytes 663560 | tf_op jit(solution)/shard_map/ppermute | solution.py:12
  24.4 14.1 %psum.7 = f32[1]{0:T(128)} all-reduce(f32[1]{0:T(128)S(6)} %convert_element_type.14), channel_id=1, replica_groups=mesh['dp'=8,'space'=16] {'dp'}, use_global_device_ids=true, to_apply=%region_0.0 | all-reduce | flops 1 | bytes 8 | tf_op jit(solution)/shard_map/psum | solution.py:44
  39.2 0.0 collective-permute-done
  39.2 0.0 collective-permute-done.1
  39.2 1.2 fusion.6
  40.4 0.1 slice_dynamic-update-slice_fusion.3
  40.5 1.0 constant_dynamic-update-slice_fusion.4
  41.5 1.0 constant_dynamic-update-slice_fusion.3
  42.5 0.0 copy-done.2
  42.5 0.1 fusion.7
  42.6 0.1 fusion.8
  42.7 0.0 collective-permute-done.2
  42.8 0.0 collective-permute-done.3
  42.8 1.2 select_maximum_fusion
  43.9 0.1 slice_dynamic-update-slice_fusion.1
  44.1 1.0 constant_dynamic-update-slice_fusion.1
  45.0 1.0 constant_dynamic-update-slice_fusion
  46.0 1.9 copy-done.3
  47.9 13.2 %fusion = f32[2048,2304]{0,1:T(8,128)} fusion(f32[]{:T(128)} %bitcast.3, bf16[1,12,72,2304]{3,2,1,0:T(8,128)(2,1)S(1)} %slice_dynamic-update-slice_fusion, bf16[1,12,72,2048]{3,2,1,0:T(8,128)(2,1)S(1)} %copy-done), kind=kOutput, calls=%fused_computation.1 | convolution fusion | flops 8158445568 | bytes 26394628 | tf_op jit(solution)/shard_map/dot_general | solution.py:48
  61.1 18.7 %copy.8 = f32[2048,2304]{1,0:T(8,128)} copy(f32[2048,2304]{0,1:T(8,128)} %fusion) | data formatting | bytes 37748736
  79.8 0.0 reduce-scatter.4.cloned.1.call-update
  79.8 17.5 %reshape.29 = bf16[2048,2304]{1,0:T(8,128)(2,1)} reshape(bf16[18432,256]{1,0:T(8,128)(2,1)} %param.6) | data formatting | bytes 18874368 | tf_op jit(solution)/shard_map/reshape | solution.py:51
  97.3 13.7 %multiply_convert_fusion = bf16[864,2048]{1,0:T(8,128)(2,1)} fusion(bf16[864,2304]{1,0:T(8,128)(2,1)} %bitcast.18, bf16[2048,2304]{1,0:T(8,128)(2,1)} %reshape.29, f32[]{:T(128)} %bitcast.3), kind=kOutput, calls=%fused_computation.2 | convolution fusion | flops 8157265920 | bytes 16957444 | tf_op jit(solution)/shard_map/dot_general | solution.py:52
  111.1 207.2 %reduce-scatter.4.cloned.1.call-done = f32[16,2304]{1,0:T(8,128)} async-done(((f32[2048,2304]{1,0:T(8,128)}), f32[16,2304]{1,0:T(8,128)}) %reduce-scatter.4.cloned.1.call-update) | async-done | bytes 147472 | tf_op jit(solution)/shard_map/reduce_scatter | solution.py:49
  318.3 1.6 reshape.27
  319.9 0.0 copy-done.1
  (7 shorter events, 0.1 us)
Async XLA Ops:
  7.2 40.7 %copy-start = (bf16[1,12,72,2048]{3,2,1,0:T(8,128)(2,1)S(1)}, bf16[1,12,72,2048]{3,2,1,0:T(8,128)(2,1)}, u32[]{:S(2)}) copy-start(bf16[1,12,72,2048]{3,2,1,0:T(8,128)(2,1)} %param.4) | copy-start | bytes 10616836
  7.2 311.1 %reduce-scatter.4.cloned.1.call-start = ((), (), s32[]{:S(2)}) async-start(), calls=%async_computation.1 | async-start | bytes 19021824 | tf_op jit(solution)/shard_map/reduce_scatter | solution.py:49
  9.2 30.0 %collective-permute-start = (bf16[1,6,72,256]{3,2,1,0:T(8,128)(2,1)}, bf16[1,6,72,256]{3,2,1,0:T(8,128)(2,1)}, u32[]{:S(2)}, u32[]{:S(2)}) collective-permute-start(bf16[1,6,72,256]{3,2,1,0:T(8,128)(2,1)} %get-tuple-element.2), channel_id=1, source_target_pairs={{1,0},{2,1},{3,2},{4,3},{5,4},{6,5},{7,6},{8,7},{9,8},{10,9},{11,1... | collective-permute-start | bytes 663560 | tf_op jit(solution)/shard_map/ppermute | solution.py:12
  10.5 28.8 %collective-permute-start.1 = (bf16[1,6,72,256]{3,2,1,0:T(8,128)(2,1)}, bf16[1,6,72,256]{3,2,1,0:T(8,128)(2,1)}, u32[]{:S(2)}, u32[]{:S(2)}) collective-permute-start(bf16[1,6,72,256]{3,2,1,0:T(8,128)(2,1)} %get-tuple-element.3), channel_id=1, source_target_pairs={{2,0},{3,1},{4,2},{5,3},{6,4},{7,5},{8,6},{9,7},{10,8},{11,9},{12,... | collective-permute-start | bytes 663560 | tf_op jit(solution)/shard_map/ppermute | solution.py:12
  11.8 31.0 %collective-permute-start.2 = (bf16[1,6,72,256]{3,2,1,0:T(8,128)(2,1)}, bf16[1,6,72,256]{3,2,1,0:T(8,128)(2,1)}, u32[]{:S(2)}, u32[]{:S(2)}) collective-permute-start(bf16[1,6,72,256]{3,2,1,0:T(8,128)(2,1)} %get-tuple-element.2), channel_id=1, source_target_pairs={{0,2},{1,3},{2,4},{3,5},{4,6},{5,7},{6,8},{7,9},{8,10},{9,11},{10,... | collective-permute-start | bytes 663560 | tf_op jit(solution)/shard_map/ppermute | solution.py:12
  20.0 22.7 %collective-permute-start.3 = (bf16[1,6,72,256]{3,2,1,0:T(8,128)(2,1)}, bf16[1,6,72,256]{3,2,1,0:T(8,128)(2,1)}, u32[]{:S(2)}, u32[]{:S(2)}) collective-permute-start(bf16[1,6,72,256]{3,2,1,0:T(8,128)(2,1)} %get-tuple-element.3), channel_id=1, source_target_pairs={{0,1},{1,2},{2,3},{3,4},{4,5},{5,6},{6,7},{7,8},{8,9},{9,10},{10,1... | collective-permute-start | bytes 663560 | tf_op jit(solution)/shard_map/ppermute | solution.py:12
  38.5 4.0 %copy-start.2 = (bf16[1,12,72,256]{3,2,1,0:T(8,128)(2,1)S(1)}, bf16[1,12,72,256]{3,2,1,0:T(8,128)(2,1)}, u32[]{:S(2)}) copy-start(bf16[1,12,72,256]{3,2,1,0:T(8,128)(2,1)} %param.5) | copy-start | bytes 1327108
  46.0 1.9 copy-start.3
  97.3 222.5 %copy-start.1 = (bf16[1,12,72,2048]{3,2,1,0:T(8,128)(2,1)S(1)}, bf16[1,12,72,2048]{3,2,1,0:T(8,128)(2,1)}, u32[]{:S(2)}) copy-start(bf16[1,12,72,2048]{3,2,1,0:T(8,128)(2,1)} %param.4) | copy-start | bytes 10616836
Sparse Core Ops, SparseCore 0:
  79.9 238.3 reduce-scatter.3

commit v2 on v1

v2 whole, which is shorter than its diff:
```python
import functools

import jax
import jax.numpy as jnp
from jax import lax
from jax.experimental import pallas as pl
from jax.experimental.pallas import tpu as pltpu
from jax.sharding import PartitionSpec as P

KERNEL_DILATION = 18
MESH = pl.DeviceIdType.MESH
F32 = jnp.float32
BF16 = jnp.bfloat16

SIDE = 4
KY_ORDER = (1, 0, 2)
WAVES = ((0, 1), (1, 2))
AXIS_ORDERS = ("xyz", "yzx", "zxy")


def body(
    cols,
    feat, grad, weight, alive,
    wg, gf,
    own_g, par_g, fb, sh, wraw, wf32, wgs, wt, acc, rb1, rb2, rb3, flags, gbuf,
    halo_s, halo_r, fwd_s, fwd_r, cen_s, cen_r, fea_s, fea_r, flag_s, flag_r, st_s, st_r, loc, gf_sem,
):
    pixels = grad.shape[0]
    half = pixels // 2
    out_channels = grad.shape[1]
    width = 3 * out_channels
    block = fb.shape[2]
    dp, space = lax.axis_index("dp"), lax.axis_index("space")
    dp_n, space_n = 2 * SIDE, SIDE * SIDE
    x, k = dp // 2, dp % 2
    z, y = space // SIDE, space % SIDE
    me = {"x": x, "y": y, "z": z}

    def dev(d, s):
        return {"dp": d, "space": s}

    def step(axis, delta):
        moved = dict(me)
        moved[axis] = lax.rem(me[axis] + (delta + SIDE), SIDE)
        return dev(2 * moved["x"] + k, SIDE * moved["z"] + moved["y"])

    def along_space(delta):
        return dev(dp, lax.rem(space + (delta + space_n), space_n))

    def along_dp(delta):
        return dev(lax.rem(dp + delta, dp_n), space)

    partner = dev(2 * x + (1 - k), space)

    barrier = pltpu.get_barrier_semaphore()
    peers = [along_dp(d) for d in range(1, dp_n)]
    peers += [along_space(d) for d in (1, -1, 2, -2)]
    peers += [step(a, d) for a in "yz" for d in (1, -1)]
    for p in peers:
        pl.semaphore_signal(barrier, inc=1, device_id=p, device_id_type=MESH)
    pl.semaphore_wait(barrier, len(peers))

    def remote(src, dst, s_sem, r_sem, to):
        return pltpu.make_async_remote_copy(
            src_ref=src, dst_ref=dst, send_sem=s_sem, recv_sem=r_sem, device_id=to, device_id_type=MESH
        )

    first, last = pl.ds(0, half), pl.ds(half, half)
    halos = [
        remote(grad.at[last], own_g.at[1, first], halo_s.at[0], halo_r.at[0], along_space(-1)),
        remote(grad.at[first], own_g.at[1, last], halo_s.at[1], halo_r.at[1], along_space(-2)),
        remote(grad.at[last], own_g.at[2, first], halo_s.at[2], halo_r.at[2], along_space(2)),
        remote(grad.at[first], own_g.at[2, last], halo_s.at[3], halo_r.at[3], along_space(1)),
    ]
    for c in halos:
        c.start()
    centre = remote(grad, par_g.at[0], cen_s, cen_r, partner)
    centre.start()
    flag_copies = [
        remote(alive, flags.at[d - 1], flag_s.at[d - 1], flag_r.at[d - 1], along_dp(d)) for d in range(1, dp_n)
    ]
    for c in flag_copies:
        c.start()

    def feature_block(v, kk):
        return feat.at[:, pl.ds(pl.multiple_of((2 * v + kk) * block, block), block)]

    own_grad = pltpu.make_async_copy(grad, own_g.at[0], loc.at[0])
    own_grad.start()
    features = []
    for v in range(SIDE):
        c = remote(feature_block(v, 1 - k), fb.at[v, pl.ds(pixels, pixels)], fea_s.at[v], fea_r.at[v], partner)
        c.start()
        own = pltpu.make_async_copy(feature_block(v, k), fb.at[v, pl.ds(0, pixels)], loc.at[2 + v])
        own.start()
        features += [c, own]
    weights = pltpu.make_async_copy(weight, wraw, loc.at[1])
    weights.start()

    pair = 2 * cols
    position = lax.broadcasted_iota(jnp.int32, (pair, out_channels), 0)
    column = jnp.where(position >= cols, position - cols, position)
    keep_low = column < cols - KERNEL_DILATION
    keep_high = column >= KERNEL_DILATION

    def build(source, base, ky, factor, start, stop):
        def rows(i, _):
            at = pl.ds(pl.multiple_of(i * pair, pair), pair)
            to = pl.ds(pl.multiple_of(base + i * pair, 16), pair)
            g = source[at, :].astype(F32) * factor
            low = jnp.where(keep_low, pltpu.roll(g, pair - KERNEL_DILATION, 0), 0.0)
            high = jnp.where(keep_high, pltpu.roll(g, KERNEL_DILATION, 0), 0.0)
            for kx, value in enumerate((low, g, high)):
                t = 3 * ky + kx
                sh[to, t * out_channels : (t + 1) * out_channels] = value.astype(BF16)
            return 0

        lax.fori_loop(start, stop, rows, 0)

    pairs = pixels // pair

    own_flag = alive[0:1, 0:1]

    def inside(delta):
        there = space + delta
        return jnp.where((there >= 0) & (there < space_n), 1.0, 0.0)

    def build_halo(source, base, ky, flag):
        low, high = (1, 2) if ky == 0 else (-2, -1)
        build(source, base, ky, flag * inside(low), 0, pairs // 2)
        build(source, base, ky, flag * inside(high), pairs // 2, pairs)

    def term(ki):
        ky = KY_ORDER[ki]

        def one(v, _):
            r = lax.dot_general(
                fb[v], sh[:, ky * width : (ky + 1) * width], (((0,), (0,)), ((), ())), preferred_element_type=F32
            )
            for kx in range(3):
                for h in range(2):
                    start = kx * out_channels + h * 128
                    acc[ki, kx, h, v] = r[:, start : start + 128].reshape(SIDE, SIDE, block // (SIDE * SIDE), 128)
            return 0

        lax.fori_loop(0, SIDE, one, 0)

    stages = (rb1, rb2, rb3)

    def view(wave, kx, h, stage, value):
        lo, n = WAVES[wave]
        order = AXIS_ORDERS[kx]
        index = {a: slice(None) for a in "xyz"}
        for done in order[:stage]:
            index[done] = me[done]
        index[order[stage]] = value
        return (pl.ds(lo, n), kx, h, index["x"], index["z"], index["y"])

    rings = {}

    def ring(wave, kx, stage):
        if (wave, kx, stage) not in rings:
            rings[wave, kx, stage] = make_ring(wave, kx, stage)
        return rings[wave, kx, stage]

    def make_ring(wave, kx, stage):
        lo, n = WAVES[wave]
        axis = AXIS_ORDERS[kx][stage]
        at = me[axis]
        nxt, two, prv = (lax.rem(at + d, SIDE) for d in (1, 2, 3))
        sends = [(0, two, 1), (1, nxt, 1), (0, nxt, 1), (1, two, -1), (0, prv, -1), (1, prv, -1)]
        copies = []
        for m, (h, value, way) in enumerate(sends):
            copies.append(
                remote(
                    acc.at[view(wave, kx, h, stage, value)],
                    stages[stage].at[pl.ds(lo, n), kx, m],
                    st_s.at[wave, kx, stage, m],
                    st_r.at[wave, kx, stage, m],
                    step(axis, way),
                )
            )
        return copies

    def begin(wave, stage):
        for kx in range(3):
            c = ring(wave, kx, stage)
            for m in (0, 3, 1, 4):
                c[m].start()

    def middle(wave, stage):
        lo, n = WAVES[wave]
        buf = stages[stage]
        for kx in range(3):
            axis = AXIS_ORDERS[kx][stage]
            c = ring(wave, kx, stage)
            for arrived, onward, h, delta in ((0, 2, 0, 1), (3, 5, 1, 3)):
                c[arrived].wait_recv()
                at = view(wave, kx, h, stage, lax.rem(me[axis] + delta, SIDE))
                acc[at] = acc[at] + buf[pl.ds(lo, n), kx, arrived]
                c[onward].start()

    def finish(wave, stage):
        lo, n = WAVES[wave]
        buf = stages[stage]
        for kx in range(3):
            axis = AXIS_ORDERS[kx][stage]
            c = ring(wave, kx, stage)
            for h, parts in ((0, (4, 2)), (1, (1, 5))):
                for m in parts:
                    c[m].wait_recv()
                at = view(wave, kx, h, stage, me[axis])
                got = [buf[pl.ds(lo, n), kx, m] for m in parts]
                total = acc[at] + got[0] + got[1]
                if stage < 2:
                    acc[at] = total
                else:
                    total = total * inverse
                    for i in range(n):
                        t = 3 * KY_ORDER[lo + i] + kx
                        wgs[h, pl.ds(t, 16, 9), :] = total[i]

    def drain():
        for wave in range(len(WAVES)):
            for stage in range(3):
                for kx in range(3):
                    for c in ring(wave, kx, stage):
                        c.wait_send()

    chans = wf32.shape[1] // 9

    def relayout(i0, i1):
        def one(i, _):
            at = pl.ds(pl.multiple_of(i * chans * 9, 16), chans * 9)
            for h in range(out_channels // 128):
                wf32[h] = wraw[at, h * 128 : (h + 1) * 128].astype(F32)
            to = pl.ds(pl.multiple_of(i * chans, 16), chans)
            for t in range(9):
                for h in range(out_channels // 128):
                    piece = wf32[h, pl.ds(t, chans, 9), :]
                    lane = t * out_channels + h * 128
                    wt[to, lane : lane + 128] = piece.astype(BF16)
            return 0

        lax.fori_loop(i0, i1, one, 0)

    gblock = gbuf.shape[2]
    gcount = gf.shape[1] // gblock

    def gf_copy(b):
        return pltpu.make_async_copy(
            gbuf.at[b % 2], gf.at[:, pl.ds(pl.multiple_of(b * gblock, gblock), gblock)], gf_sem.at[b % 2]
        )

    def back(b0, b1):
        for b in range(b0, b1):
            if b >= 2:
                gf_copy(b - 2).wait()
            r = lax.dot_general(
                sh[0:pixels, :], wt[pl.ds(b * gblock, gblock), :], (((1,), (1,)), ((), ())), preferred_element_type=F32
            )
            gbuf[b % 2] = (r * inverse[0:1, 0:1]).astype(BF16)
            gf_copy(b).start()

    blocks = wt.shape[0] // chans
    own_grad.wait()
    build(own_g.at[0], 0, 1, own_flag, 0, pairs)
    for c in flag_copies:
        c.wait_recv()
    total = alive[...]
    for d in range(1, dp_n):
        total = total + flags[d - 1]
    inverse = (1.0 / total)[0:1, :]
    par_flag = flags[6 * (1 - k)][0:1, 0:1]
    centre.wait_recv()
    build(par_g.at[0], pixels, 1, par_flag, 0, pairs)
    for i, c in enumerate(features):
        if i % 2:
            c.wait()
        else:
            c.wait_recv()
    term(0)
    begin(0, 0)
    forwards = []
    for i, c in enumerate(halos):
        c.wait_recv()
        where = (1 + i // 2, first if i % 2 == 0 else last)
        f = remote(own_g.at[where], par_g.at[where], fwd_s.at[i], fwd_r.at[i], partner)
        f.start()
        forwards.append(f)
    build_halo(own_g.at[1], 0, 0, own_flag)
    build_halo(own_g.at[2], 0, 2, own_flag)
    for f in forwards:
        f.wait_recv()
    build_halo(par_g.at[1], pixels, 0, par_flag)
    build_halo(par_g.at[2], pixels, 2, par_flag)
    middle(0, 0)
    term(1)
    term(2)
    begin(1, 0)
    finish(0, 0)
    begin(0, 1)
    weights.wait()
    relayout(0, blocks // 2)
    middle(0, 1)
    relayout(blocks // 2, blocks)
    middle(1, 0)
    finish(0, 1)
    begin(0, 2)
    back(0, 2)
    middle(0, 2)
    back(2, 4)
    finish(1, 0)
    begin(1, 1)
    finish(0, 2)
    back(4, 6)
    middle(1, 1)
    back(6, 7)
    finish(1, 1)
    begin(1, 2)
    back(7, gcount)
    middle(1, 2)
    finish(1, 2)
    for h in range(out_channels // 128):
        wg[:, h * 128 : (h + 1) * 128] = wgs[h]
    gf_copy(gcount - 2).wait()
    gf_copy(gcount - 1).wait()
    for c in halos + [centre] + flag_copies + forwards:
        c.wait_send()
    for c in features[::2]:
        c.wait_send()
    drain()


def fused(features, grad_out, weight, alive):
    members, rows, cols, in_channels = features.shape
    out_channels = grad_out.shape[-1]
    pixels = rows * cols
    block = in_channels // (2 * SIDE)
    sub = block // 16
    chans = 128
    gblock = 256
    dma = pltpu.SemaphoreType.DMA
    anyspace = pl.BlockSpec(memory_space=pl.ANY)
    vmem = pl.BlockSpec(memory_space=pltpu.VMEM)
    scratch = [
        pltpu.VMEM((3, pixels, out_channels), BF16),
        pltpu.VMEM((3, pixels, out_channels), BF16),
        pltpu.VMEM((SIDE, 2 * pixels, block), BF16),
        pltpu.VMEM((2 * pixels, 9 * out_channels), BF16),
        pltpu.VMEM(weight.shape, BF16),
        pltpu.VMEM((out_channels // 128, 9 * chans, 128), F32),
        pltpu.VMEM((out_channels // 128, sub * 9, 128), F32),
        pltpu.VMEM((in_channels, 9 * out_channels), BF16),
        pltpu.VMEM((3, 3, 2, SIDE, SIDE, SIDE, sub, 128), F32),
        pltpu.VMEM((3, 3, 6, SIDE, SIDE, sub, 128), F32),
        pltpu.VMEM((3, 3, 6, SIDE, sub, 128), F32),
        pltpu.VMEM((3, 3, 6, sub, 128), F32),
        pltpu.VMEM((2 * SIDE - 1, 8, 128), F32),
        pltpu.VMEM((2, pixels, gblock), BF16),
        dma((4,)), dma((4,)), dma((4,)), dma((4,)), dma(()), dma(()), dma((SIDE,)), dma((SIDE,)),
        dma((2 * SIDE - 1,)), dma((2 * SIDE - 1,)),
        dma((len(WAVES), 3, 3, 6)), dma((len(WAVES), 3, 3, 6)), dma((2 + SIDE,)), dma((2,)),
    ]
    flag = jnp.broadcast_to(alive.astype(F32).reshape(1, 1), (8, 128))
    weight_grad, grad_features = pl.pallas_call(
        functools.partial(body, cols),
        out_shape=(
            jax.ShapeDtypeStruct((sub * 9, out_channels), F32),
            jax.ShapeDtypeStruct((pixels, in_channels), BF16),
        ),
        in_specs=[anyspace, anyspace, anyspace, vmem],
        out_specs=(vmem, anyspace),
        scratch_shapes=scratch,
        compiler_params=pltpu.CompilerParams(
            collective_id=0, has_side_effects=True, vmem_limit_bytes=66_000_000
        ),
    )(features.reshape(pixels, in_channels), grad_out.reshape(pixels, out_channels), weight, flag)
    return weight_grad, grad_features.reshape(features.shape)


def solution(mesh):
    in_specs = (P("dp", "space", None, None), P("dp", "space", None, None), P(), P("dp"))
    out_specs = (P(("dp", "space"), None), P("dp", "space", None, None))
    return jax.shard_map(fused, mesh=mesh, in_specs=in_specs, out_specs=out_specs, check_vma=False)
```

time: 328 us -> 92.1 us (0.28)
  waiting for transfers between devices: 207 us -> 0 us
  Pallas kernels: 0 us -> 84.2 us
  local copies, waits for them, and re-layouts: 46 us -> 6.45 us
  matrix products: 26.9 us -> 0 us
  starting transfers between devices: 14.6 us -> 0 us
  between operations: 15.6 us -> 1.29 us
  blocking collectives: 14.1 us -> 0 us
    reduce_scatter x1 -> x0, waiting for transfers between devices: 207 us -> none  [shards(): lax.psum_scatter(term * scale, ('dp', 'space'), scatter_dimension=0, tile...]
    pallas_call x0 -> x1, Pallas kernels: none -> 84.2 us  [fused(): pl.pallas_call(functools.partial(body, cols), out_shape=(jax.ShapeDtypeSt...]
    dot_general x2 -> x0, matrix products: 26.9 us -> none  [the longest x1 13.7 us: shards(): lax.dot_general(taps, kernel, (((1,), (1,)), ((), ())), preferred_element...]
    reshape x2 -> x0, local copies, waits for them, and re-layouts: 19.1 us -> none  [the longest x1 17.5 us: shards(): kernel = weight.reshape(in_channels, 9 * out_channels)]
    unnamed x19 -> x2, local copies, waits for them, and re-layouts: 24.8 us -> 5.85 us
    ppermute x4 -> x0, starting transfers between devices: 14.6 us -> none  [from_behind(): lax.ppermute(value, axis, [(source, source + steps) for source in range(l...]
    psum x1 -> x0, blocking collectives: 14.1 us -> none  [shards(): survivors = lax.psum(jnp.sum(alive).astype(jnp.float32), 'dp')]
  transfers between devices with their start and end apart: 5 -> 0, of which waited for: 1 -> 0; matrix products, arithmetic and copies ran while one was open for 11% -> 0% of each run, Pallas kernels for 0% -> 0%
where the time goes in v2:
time: 92.1 us; the launch traced here: 91.9 us
  Pallas kernels  84.2 us (91%)
  local copies, waits for them, and re-layouts  6.45 us (7%)
  between operations  1.29 us (1%)
    pallas_call x1, Pallas kernels, fused(): pl.pallas_call(functools.partial(body, cols), out_shape=(jax.ShapeDtypeSt...  84.2 us
    unnamed x2, local copies, waits for them, and re-layouts  5.85 us

profile of v2, /device:TPU:0, one launch (start us, length us, event | category | flops | bytes accessed | tf_op | source)
XLA Modules:
  0.0 91.9 jit_solution(17915055211174974036)
XLA Ops:
  1.3 0.6 broadcast_in_dim.8.alive
  1.9 84.2 %shard_map.59 = (f32[144,256]{1,0:T(8,128)}, bf16[864,2048]{1,0:T(8,128)(2,1)}) custom-call(bf16[864,2048]{1,0:T(8,128)(2,1)} %bitcast.4, bf16[864,256]{1,0:T(8,128)(2,1)} %bitcast.6, bf16[18432,256]{1,0:T(8,128)(2,1)} %weight.1, f32[8,128]{1,0:T(8,128)} %broadcast_in_dim.8.alive), custom_call_target="tpu_custom_call" | custom-call | tf_op jit(solution)/shard_map/pallas_call | solution.py:366
  86.1 1.6 %copy.9 = f32[144,256]{1,0:T(8,128)} copy(f32[144,256]{1,0:T(8,128)} %get-tuple-element.8) | data formatting | bytes 294912
  87.7 4.3 %copy.10 = bf16[1,12,72,2048]{3,2,1,0:T(8,128)(2,1)} copy(bf16[1,12,72,2048]{3,2,1,0:T(8,128)(2,1)} %bitcast.5) | data formatting | bytes 7077888

commit v3 on v2

--- a/solution.py
+++ b/solution.py
@@ -14,7 +14,7 @@
 
 SIDE = 4
 KY_ORDER = (1, 0, 2)
-WAVES = ((0, 1), (1, 2))
+WAVES = ((0, 1), (1, 1), (2, 1))
 AXIS_ORDERS = ("xyz", "yzx", "zxy")
 
 
@@ -58,6 +58,55 @@
     peers += [step(a, d) for a in "yz" for d in (1, -1)]
     for p in peers:
         pl.semaphore_signal(barrier, inc=1, device_id=p, device_id_type=MESH)
+
+    def feature_block(v, kk):
+        return feat.at[:, pl.ds(pl.multiple_of((2 * v + kk) * block, block), block)]
+
+    own_grad = pltpu.make_async_copy(grad, own_g.at[0], loc.at[0])
+    own_grad.start()
+    own_features = [
+        pltpu.make_async_copy(feature_block(v, k), fb.at[v, pl.ds(0, pixels)], loc.at[2 + v]) for v in range(SIDE)
+    ]
+    for c in own_features:
+        c.start()
+    weights = pltpu.make_async_copy(weight, wraw, loc.at[1])
+    weights.start()
+
+    pair = 2 * cols
+    position = lax.broadcasted_iota(jnp.int32, (pair, out_channels), 0)
+    column = jnp.where(position >= cols, position - cols, position)
+    keep_low = column < cols - KERNEL_DILATION
+    keep_high = column >= KERNEL_DILATION
+
+    def build(source, base, ky, factor, start, stop):
+        def rows(i, _):
+            at = pl.ds(pl.multiple_of(i * pair, pair), pair)
+            to = pl.ds(pl.multiple_of(base + i * pair, 16), pair)
+            g = source[at, :].astype(F32) * factor
+            low = jnp.where(keep_low, pltpu.roll(g, pair - KERNEL_DILATION, 0), 0.0)
+            high = jnp.where(keep_high, pltpu.roll(g, KERNEL_DILATION, 0), 0.0)
+            for kx, value in enumerate((low, g, high)):
+                t = 3 * ky + kx
+                sh[to, t * out_channels : (t + 1) * out_channels] = value.astype(BF16)
+            return 0
+
+        lax.fori_loop(start, stop, rows, 0)
+
+    pairs = pixels // pair
+
+    own_flag = alive[0:1, 0:1]
+
+    def inside(delta):
+        there = space + delta
+        return jnp.where((there >= 0) & (there < space_n), 1.0, 0.0)
+
+    def build_halo(source, base, ky, flag):
+        low, high = (1, 2) if ky == 0 else (-2, -1)
+        build(source, base, ky, flag * inside(low), 0, pairs // 2)
+        build(source, base, ky, flag * inside(high), pairs // 2, pairs)
+
+    own_grad.wait()
+    build(own_g.at[0], 0, 1, own_flag, 0, pairs)
     pl.semaphore_wait(barrier, len(peers))
 
     def remote(src, dst, s_sem, r_sem, to):
@@ -82,53 +131,12 @@
     for c in flag_copies:
         c.start()
 
-    def feature_block(v, kk):
-        return feat.at[:, pl.ds(pl.multiple_of((2 * v + kk) * block, block), block)]
-
-    own_grad = pltpu.make_async_copy(grad, own_g.at[0], loc.at[0])
-    own_grad.start()
-    features = []
-    for v in range(SIDE):
-        c = remote(feature_block(v, 1 - k), fb.at[v, pl.ds(pixels, pixels)], fea_s.at[v], fea_r.at[v], partner)
+    features = [
+        remote(feature_block(v, 1 - k), fb.at[v, pl.ds(pixels, pixels)], fea_s.at[v], fea_r.at[v], partner)
+        for v in range(SIDE)
+    ]
+    for c in features:
         c.start()
-        own = pltpu.make_async_copy(feature_block(v, k), fb.at[v, pl.ds(0, pixels)], loc.at[2 + v])
-        own.start()
-        features += [c, own]
-    weights = pltpu.make_async_copy(weight, wraw, loc.at[1])
-    weights.start()
-
-    pair = 2 * cols
-    position = lax.broadcasted_iota(jnp.int32, (pair, out_channels), 0)
-    column = jnp.where(position >= cols, position - cols, position)
-    keep_low = column < cols - KERNEL_DILATION
-    keep_high = column >= KERNEL_DILATION
-
-    def build(source, base, ky, factor, start, stop):
-        def rows(i, _):
-            at = pl.ds(pl.multiple_of(i * pair, pair), pair)
-            to = pl.ds(pl.multiple_of(base + i * pair, 16), pair)
-            g = source[at, :].astype(F32) * factor
-            low = jnp.where(keep_low, pltpu.roll(g, pair - KERNEL_DILATION, 0), 0.0)
-            high = jnp.where(keep_high, pltpu.roll(g, KERNEL_DILATION, 0), 0.0)
-            for kx, value in enumerate((low, g, high)):
-                t = 3 * ky + kx
-                sh[to, t * out_channels : (t + 1) * out_channels] = value.astype(BF16)
-            return 0
-
-        lax.fori_loop(start, stop, rows, 0)
-
-    pairs = pixels // pair
-
-    own_flag = alive[0:1, 0:1]
-
-    def inside(delta):
-        there = space + delta
-        return jnp.where((there >= 0) & (there < space_n), 1.0, 0.0)
-
-    def build_halo(source, base, ky, flag):
-        low, high = (1, 2) if ky == 0 else (-2, -1)
-        build(source, base, ky, flag * inside(low), 0, pairs // 2)
-        build(source, base, ky, flag * inside(high), pairs // 2, pairs)
 
     def term(ki):
         ky = KY_ORDER[ki]
@@ -182,16 +190,16 @@
             )
         return copies
 
-    def begin(wave, stage):
-        for kx in range(3):
+    def begin(wave, stage, kxs=(0, 1, 2)):
+        for kx in kxs:
             c = ring(wave, kx, stage)
             for m in (0, 3, 1, 4):
                 c[m].start()
 
-    def middle(wave, stage):
+    def middle(wave, stage, kxs=(0, 1, 2)):
         lo, n = WAVES[wave]
         buf = stages[stage]
-        for kx in range(3):
+        for kx in kxs:
             axis = AXIS_ORDERS[kx][stage]
             c = ring(wave, kx, stage)
             for arrived, onward, h, delta in ((0, 2, 0, 1), (3, 5, 1, 3)):
@@ -263,8 +271,6 @@
             gf_copy(b).start()
 
     blocks = wt.shape[0] // chans
-    own_grad.wait()
-    build(own_g.at[0], 0, 1, own_flag, 0, pairs)
     for c in flag_copies:
         c.wait_recv()
     total = alive[...]
@@ -274,13 +280,14 @@
     par_flag = flags[6 * (1 - k)][0:1, 0:1]
     centre.wait_recv()
     build(par_g.at[0], pixels, 1, par_flag, 0, pairs)
-    for i, c in enumerate(features):
-        if i % 2:
-            c.wait()
-        else:
-            c.wait_recv()
+    for c in own_features:
+        c.wait()
+    for c in features:
+        c.wait_recv()
     term(0)
-    begin(0, 0)
+    begin(0, 0, (0, 2))
+    weights.wait()
+    relayout(0, 5)
     forwards = []
     for i, c in enumerate(halos):
         c.wait_recv()
@@ -288,46 +295,60 @@
         f = remote(own_g.at[where], par_g.at[where], fwd_s.at[i], fwd_r.at[i], partner)
         f.start()
         forwards.append(f)
+    begin(0, 0, (1,))
     build_halo(own_g.at[1], 0, 0, own_flag)
     build_halo(own_g.at[2], 0, 2, own_flag)
-    for f in forwards:
+    middle(0, 0, (0, 2))
+    for f in forwards[:2]:
         f.wait_recv()
     build_halo(par_g.at[1], pixels, 0, par_flag)
+    term(1)
+    begin(1, 0)
+    for f in forwards[2:]:
+        f.wait_recv()
     build_halo(par_g.at[2], pixels, 2, par_flag)
-    middle(0, 0)
-    term(1)
     term(2)
-    begin(1, 0)
+    begin(2, 0)
+    middle(0, 0, (1,))
+    relayout(5, 8)
+    middle(1, 0)
     finish(0, 0)
     begin(0, 1)
-    weights.wait()
-    relayout(0, blocks // 2)
+    relayout(8, 12)
     middle(0, 1)
-    relayout(blocks // 2, blocks)
-    middle(1, 0)
+    relayout(12, 14)
+    middle(2, 0)
+    finish(1, 0)
+    begin(1, 1)
+    relayout(14, blocks)
     finish(0, 1)
     begin(0, 2)
-    back(0, 2)
+    back(0, 1)
+    middle(1, 1)
+    finish(2, 0)
+    begin(2, 1)
     middle(0, 2)
-    back(2, 4)
-    finish(1, 0)
-    begin(1, 1)
-    finish(0, 2)
-    back(4, 6)
-    middle(1, 1)
-    back(6, 7)
+    back(1, 3)
     finish(1, 1)
     begin(1, 2)
-    back(7, gcount)
+    middle(2, 1)
+    finish(0, 2)
+    back(3, 5)
+    finish(2, 1)
+    begin(2, 2)
     middle(1, 2)
+    back(5, 6)
+    middle(2, 2)
     finish(1, 2)
+    back(6, gcount)
+    finish(2, 2)
     for h in range(out_channels // 128):
         wg[:, h * 128 : (h + 1) * 128] = wgs[h]
     gf_copy(gcount - 2).wait()
     gf_copy(gcount - 1).wait()
     for c in halos + [centre] + flag_copies + forwards:
         c.wait_send()
-    for c in features[::2]:
+    for c in features:
         c.wait_send()
     drain()
 

time: 92.1 us -> 90.7 us (0.985)
  Pallas kernels: 84.2 us -> 82.7 us
    pallas_call x1, Pallas kernels: 84.2 us -> 82.7 us  [fused(): pl.pallas_call(functools.partial(body, cols), out_shape=(jax.ShapeDtypeSt...]
where the time goes in v3:
time: 90.7 us; the launch traced here: 90.5 us
  Pallas kernels  82.7 us (91%)
  local copies, waits for them, and re-layouts  6.45 us (7%)
  between operations  1.29 us (1%)
    pallas_call x1, Pallas kernels, fused(): pl.pallas_call(functools.partial(body, cols), out_shape=(jax.ShapeDtypeSt...  82.7 us
    unnamed x2, local copies, waits for them, and re-layouts  5.85 us

profile of v3, /device:TPU:0, one launch (start us, length us, event | category | flops | bytes accessed | tf_op | source)
XLA Modules:
  0.0 90.5 jit_solution(13521352761138191441)
XLA Ops:
  1.3 0.6 broadcast_in_dim.8.alive
  1.9 82.7 %shard_map.59 = (f32[144,256]{1,0:T(8,128)}, bf16[864,2048]{1,0:T(8,128)(2,1)}) custom-call(bf16[864,2048]{1,0:T(8,128)(2,1)} %bitcast.4, bf16[864,256]{1,0:T(8,128)(2,1)} %bitcast.6, bf16[18432,256]{1,0:T(8,128)(2,1)} %weight.1, f32[8,128]{1,0:T(8,128)} %broadcast_in_dim.8.alive), custom_call_target="tpu_custom_call" | custom-call | tf_op jit(solution)/shard_map/pallas_call | solution.py:387
  84.6 1.6 %copy.9 = f32[144,256]{1,0:T(8,128)} copy(f32[144,256]{1,0:T(8,128)} %get-tuple-element.8) | data formatting | bytes 294912
  86.2 4.3 %copy.10 = bf16[1,12,72,2048]{3,2,1,0:T(8,128)(2,1)} copy(bf16[1,12,72,2048]{3,2,1,0:T(8,128)(2,1)} %bitcast.5) | data formatting | bytes 7077888
